TPU v7x, 32 devices: a whole 2x2x4 slice. The times are simulated.
32 devices in a mesh: grp: 2 (over y), chan: 4 (over z), sub: 4 (over x, core).
Axes of the slice: x: 2, y: 2, z: 4, core: 2. Of those that a mesh axis runs over, the one named last changes fastest.
Arguments:
- voltages: bfloat16 [2048, 2, 5504], P(('grp', 'chan', 'sub')), parts along dimension 0, may hold values from -6 to 6
- taps: float32 [1536], replicated, may hold values from -0.15625 to 0.15625
- input_id: int32 [1024], replicated, may hold values from 0 to 1023, each once
- counts: int32 [8], P('grp'), parts along dimension 0, may hold values from 2 to 8, as said below
- delays: int32 [512, 1024], P(('grp', 'sub')), parts along dimension 0, may hold values from 0 to 127
- beam_owner: int32 [512, 1], P('grp'), parts along dimension 0, may hold values from 0 to 3; in each aligned block of 64 rows (0 to 63, 64 to 127, ...) at most 32 rows name the same one
Outputs:
- visibility: bfloat16 [256, 2, 1024, 1024], P(('grp', 'chan'), None, 'sub'), parts along dimension 0
- resynth: float32 [1024, 2, 5504], P(('grp', 'chan', 'sub')), parts along dimension 0
There are 2 independent parts, one for each index of `grp`. A program takes and returns all parts, laid end to end along the dimension named above; an argument that names none is the same for every part. Nothing has to cross between parts.
Inputs may be any that keep to these rules, and one draw needn't show every extreme that they name: `input_id`: each input id appears once. `counts`: every draw has a block with all 8 spectra valid. `beam_owner`: within each section of 64 consecutive beams no owner is named more than 32 times; some owner is named exactly 32 times in some section.
All inputs are finite; a program needn't handle non-finite values.
Results may differ from a plain program's by a relative error of at most 0.007.
Values may be sent and summed in bfloat16 or wider, within the bound.
A program may use at most 192 MiB of HBM per device.

v0:
```python
import math
import jax
import jax.numpy as jnp
from jax import lax
from jax.sharding import PartitionSpec as P

NCH = 128
TAPS = 12
SPEC = 8
BLOCKS = 4
BEAMS = 256


def filter_table(taps, chans):
    length = taps.shape[0]
    position = jnp.arange(length, dtype=jnp.int32) % chans
    channel = jnp.arange(chans, dtype=jnp.int32)
    phase = (position[:, None] * channel[None, :] % chans).astype(jnp.float32) * (
        2.0 * math.pi / chans
    )
    cosine = taps[:, None] * jnp.cos(phase)
    sine = taps[:, None] * jnp.sin(phase)
    upper = jnp.concatenate([cosine, -sine], axis=1)
    lower = jnp.concatenate([sine, cosine], axis=1)
    return jnp.concatenate([upper, lower], axis=0).astype(jnp.bfloat16)


def resynthesize(received, table, taps_count, chans):
    count = received.shape[0]
    spectra_n = received.shape[3]
    table3 = table.reshape(2 * taps_count * chans, 2, chans)
    grid = jnp.einsum("pcht,mch->ptm", received, table3, preferred_element_type=jnp.float32)
    grid = grid.reshape(count, spectra_n, 2, taps_count, chans)
    total = jnp.zeros((count, spectra_n + taps_count - 1, 2, chans), jnp.float32)
    for k in range(taps_count):
        total = total + jnp.pad(
            grid[:, :, :, k, :], ((0, 0), (k, taps_count - 1 - k), (0, 0), (0, 0))
        )
    return jnp.transpose(total, (0, 2, 1, 3)).reshape(
        count, 2, (spectra_n + taps_count - 1) * chans
    )


def local(voltages, taps, input_id, counts, delays, beam_owner):
    n_chan = lax.axis_size("chan")
    n_sub = lax.axis_size("sub")
    inp_dev = voltages.shape[0]
    inputs = input_id.shape[0]
    chans = NCH
    taps_count = TAPS
    spectra_n = BLOCKS * SPEC
    ch_dev = chans // n_chan
    rows = inputs // n_sub
    section = BEAMS // n_sub
    most = min(section, max(2, 2 * section // n_chan))
    table = filter_table(taps, chans)
    position = jnp.arange(spectra_n, dtype=jnp.int32)
    valid = (position % SPEC < jnp.repeat(counts, SPEC)).astype(jnp.float32)
    total = jnp.sum(counts.astype(jnp.float32))
    frames = voltages.reshape(inp_dev, 2, spectra_n + taps_count - 1, chans)
    windows = jnp.concatenate(
        [frames[:, :, k : k + spectra_n, :] for k in range(taps_count)], axis=3
    )
    table3 = table.reshape(2, taps_count * chans, 2 * chans)
    filtered = jnp.einsum("icth,chm->mit", windows, table3, preferred_element_type=jnp.float32)
    filtered = filtered * valid[None, None, :]
    spectra = filtered.reshape(2, chans, inp_dev, spectra_n).astype(jnp.bfloat16)
    slot_of = jnp.zeros((inputs,), jnp.int32).at[input_id].set(jnp.arange(inputs, dtype=jnp.int32))
    turned = lax.all_to_all(spectra, "chan", split_axis=1, concat_axis=2, tiled=True)
    gathered = lax.all_gather(turned, "sub", axis=2, tiled=True)
    chan_part = slot_of // (n_sub * inp_dev)
    sub_part = slot_of // inp_dev % n_sub
    order = (sub_part * n_chan + chan_part) * inp_dev + slot_of % inp_dev
    by_id = jnp.take(gathered, order, axis=2)
    sub_index = lax.axis_index("sub")
    mine = lax.dynamic_slice_in_dim(by_id, sub_index * rows, rows, 2)
    real_part = jnp.einsum("cxit,cxjt->xij", mine, by_id, preferred_element_type=jnp.float32)
    imag_part = jnp.einsum("xit,xjt->xij", mine[1], by_id[0], preferred_element_type=jnp.float32)
    imag_part = imag_part - jnp.einsum(
        "xit,xjt->xij", mine[0], by_id[1], preferred_element_type=jnp.float32
    )
    visibility = (jnp.stack([real_part, imag_part], axis=1) / total).astype(jnp.bfloat16)
    channel = lax.axis_index("chan") * ch_dev + jnp.arange(ch_dev, dtype=jnp.int32)
    phase = (delays[None, :, :] * channel[:, None, None] % chans).astype(jnp.float32) * (
        2.0 * math.pi / chans
    )
    scale = 1.0 / math.sqrt(inputs)
    weight_cos = (jnp.cos(phase) * scale).astype(jnp.bfloat16)
    weight_sin = (jnp.sin(phase) * scale).astype(jnp.bfloat16)
    from_cos = jnp.einsum("xbi,cxit->cxbt", weight_cos, by_id, preferred_element_type=jnp.float32)
    from_sin = jnp.einsum("xbi,cxit->cxbt", weight_sin, by_id, preferred_element_type=jnp.float32)
    beams = jnp.stack([from_cos[0] - from_sin[1], from_cos[1] + from_sin[0]]).astype(jnp.bfloat16)
    owner = lax.dynamic_slice_in_dim(beam_owner[:, 0], sub_index * section, section)
    beam = jnp.arange(section, dtype=jnp.int32)
    earlier = (owner[None, :] == owner[:, None]) & (beam[None, :] < beam[:, None])
    rank = jnp.sum(earlier.astype(jnp.int32), axis=1)
    target = owner * most + rank
    select = (jnp.arange(n_chan * most, dtype=jnp.int32)[:, None] == target[None, :]).astype(
        jnp.bfloat16
    )
    placed = jnp.einsum("pb,cxbt->pcxt", select, beams, preferred_element_type=jnp.float32).astype(
        jnp.bfloat16
    )
    placed = placed.reshape(n_chan, most, 2, ch_dev, spectra_n)
    resynth = resynthesize(
        lax.all_to_all(placed, "chan", split_axis=0, concat_axis=3, tiled=True)[0],
        table,
        taps_count,
        chans,
    )
    return (visibility, resynth)


def solution(mesh):
    placed = (
        P(("grp", "chan", "sub"), None, None),
        P(),
        P(),
        P("grp"),
        P(("grp", "sub"), None),
        P("grp", None),
    )
    return jax.shard_map(
        local,
        mesh=mesh,
        in_specs=placed,
        out_specs=(P(("grp", "chan"), None, "sub", None), P(("grp", "chan", "sub"), None, None)),
        check_vma=False,
    )
```

profile of v0, /device:TPU:0, one launch (start us, length us, event | category | flops | bytes accessed | tf_op | source)
XLA Modules:
  0.0 464.1 jit_solution(4813590015660750824)
XLA Ops:
  8.0 3.7 reshape.232
  16.0 4.7 %negate_convert_fusion.1 = (bf16[1536,128]{1,0:T(8,128)(2,1)S(1)}, bf16[1536,128]{1,0:T(8,128)(2,1)S(1)}, bf16[1536,128]{1,0:T(8,128)(2,1)S(1)}) fusion(s32[1536]{0:T(1024)S(1)} %add_select_fusion.3, f32[1536]{0:T(1024)S(1)} %copy-done.4), kind=kLoop, calls=%fused_computation.79 | loop fusion | flops 3932160 | bytes 1191936 | tf_op jit(solution)/shard_map/convert.13
  30.2 4.8 %copy-done.3 = bf16[64,2,32,1536]{3,0,1,2:T(8,128)(2,1)} copy-done((bf16[64,2,32,1536]{3,0,1,2:T(8,128)(2,1)}, bf16[64,2,32,1536]{3,0,1,2:T(8,128)(2,1)S(1)}, u32[]{:S(2)}) %copy-start.3) | copy-done | bytes 12582936
  35.1 8.2 %fusion.15 = bf16[256,64,32]{0,1,2:T(8,128)(2,1)S(1)} fusion(bf16[2,1536,256,1]{2,1,0,3:T(8,128)(2,1)S(1)} %bitcast.153, bf16[64,2,32,1536]{3,0,1,2:T(8,128)(2,1)} %copy-done.3, f32[32]{0:T(128)S(1)} %compare_convert_fusion), kind=kOutput, calls=%fused_computation.28 | convolution fusion | flops 3222274048 | bytes 15204480 | tf_op jit(solution)/shard_map/icth,chm->mit/dot_general | solution.py:65
  47.5 32.0 %all_to_all.33 = bf16[4,2,65536]{2,1,0:T(2,128)(2,1)} all-to-all(bf16[4,2,65536]{2,1,0:T(2,128)(2,1)S(1)} %reshape.237), channel_id=1, replica_groups=mesh['grp'=2,'chan'=4,'sub'=4] {'chan'}, dimensions={0} | all-to-all | bytes 2097152 | tf_op jit(solution)/shard_map/all_to_all | solution.py:69
  82.6 6.5 %copy.149 = bf16[2,32,4,64,32]{4,1,3,2,0:T(8,128)(2,1)} copy(bf16[2,32,4,64,32]{3,4,0,1,2:T(8,128)(2,1)S(1)} %bitcast.149) | data formatting | bytes 2097152 | tf_op jit(solution)/shard_map/all_to_all | solution.py:69
  89.2 4.3 scatter_custom_fusion
  94.5 4.2 negate_convert_fusion
  99.9 94.3 %all-gather.2.cloned.1.call-done = bf16[2,32,1024,32]{3,1,2,0:T(8,128)(2,1)} async-done(((bf16[2,32,256,32]{3,1,2,0:T(8,128)(2,1)}), bf16[2,32,1024,32]{3,1,2,0:T(8,128)(2,1)}) %all-gather.2.cloned.1.call-update) | async-done | bytes 4194320 | tf_op jit(solution)/shard_map/all_gather | solution.py:70
  194.3 19.1 %gather_fusion = bf16[1024,2,32,32]{3,2,1,0:T(8,128)(2,1)} fusion(bf16[2,32,1024,32]{3,1,2,0:T(8,128)(2,1)} %all-gather.2.cloned.1.call-done, s32[1024]{0:T(1024)S(1)} %broadcast_clamp_fusion), kind=kCustom, calls=%fused_computation | custom fusion | bytes 8392704 | tf_op jit(solution)/shard_map/jit(_take)/gather | solution.py:74
  213.4 17.5 %copy.109 = bf16[1024,2,32,32]{0,3,1,2:T(8,128)(2,1)} copy(bf16[1024,2,32,32]{3,2,1,0:T(8,128)(2,1)} %gather_fusion) | data formatting | bytes 8388608 | tf_op jit(solution)/shard_map/jit(_take)/gather | solution.py:74
  237.0 31.8 %fusion.21 = f32[2,32,64,32]{2,3,0,1:T(8,128)S(1)} fusion(s32[32]{0:T(128)S(1)} %iota_add_fusion, s32[64,1024]{1,0:T(8,128)S(1)} %copy-done.8, bf16[1024,2,32,32]{0,3,1,2:T(8,128)(2,1)S(1)} %broadcast_select_fusion), kind=kOutput, calls=%fused_computation.35 | convolution fusion | flops 301989888 | bytes 4980864 | tf_op jit(solution)/shard_map/xbi,cxit->cxbt/dot_general | solution.py:90
  268.8 32.1 %fusion.18 = f32[2,32,64,32]{2,3,0,1:T(8,128)S(1)} fusion(s32[32]{0:T(128)S(1)} %iota_add_fusion, s32[64,1024]{1,0:T(8,128)S(1)} %copy-done.8, bf16[1024,2,32,32]{0,3,1,2:T(8,128)(2,1)S(1)} %broadcast_select_fusion), kind=kOutput, calls=%fused_computation.34 | convolution fusion | flops 301989888 | bytes 4980864 | tf_op jit(solution)/shard_map/xbi,cxit->cxbt/dot_general | solution.py:91
  307.3 4.5 reshape.239
  311.8 4.6 all-to-all-start.1
  316.4 15.5 %convolution_bitcast_fusion = f32[32,1,256,1024]{3,2,0,1:T(8,128)} fusion(bf16[2,32,256,32]{2,3,0,1:T(8,128)(2,1)S(1)} %dynamic-slice_bitcast_fusion, bf16[1024,2,32,32]{0,3,1,2:T(8,128)(2,1)} %copy-done.1), kind=kOutput, calls=%fused_computation.8 | convolution fusion | flops 1073741824 | bytes 38797312 | tf_op jit(solution)/shard_map/cxit,cxjt->xij/dot_general | solution.py:77
  331.8 14.0 %fusion.14 = f32[32,256,1024]{2,1,0:T(8,128)} fusion(bf16[2,32,1024,32]{2,3,0,1:T(8,128)(2,1)S(1)} %copy-done.2, bf16[2,32,256,32]{2,3,0,1:T(8,128)(2,1)S(1)} %dynamic-slice_bitcast_fusion), kind=kOutput, calls=%fused_computation.26 | convolution fusion | flops 536870912 | bytes 36175872 | tf_op jit(solution)/shard_map/xit,xjt->xij/dot_general | solution.py:78
  345.9 21.7 %subtract_bitcast_fusion = f32[32,1,256,1024]{3,2,0,1:T(8,128)} fusion(f32[32,256,1024]{2,1,0:T(8,128)} %fusion.14, bf16[2,32,1024,32]{2,3,0,1:T(8,128)(2,1)S(1)} %copy-done.2, bf16[2,32,256,32]{2,3,0,1:T(8,128)(2,1)S(1)} %dynamic-slice_bitcast_fusion), kind=kOutput, calls=%fused_computation.4 | convolution fusion | flops 545259520 | bytes 69730304 | tf_op jit(solution)/shard_map/xit,xjt->xij/dot_general | solution.py:79
  367.5 33.5 %fusion = bf16[32,2,256,1024]{3,2,0,1:T(8,128)(2,1)} fusion(f32[32,1,256,1024]{3,2,0,1:T(8,128)} %subtract_bitcast_fusion, f32[32,1,256,1024]{3,2,0,1:T(8,128)} %convolution_bitcast_fusion, f32[]{:T(128)} %convert_reduce_fusion.1), kind=kLoop, calls=%fused_computation.3 | loop fusion | flops 50331648 | bytes 100663296 | tf_op jit(solution)/shard_map/convert_element_type | solution.py:82
  401.1 23.2 %copy.126 = bf16[32,2,256,1024]{3,2,1,0:T(8,128)(2,1)} copy(bf16[32,2,256,1024]{3,2,0,1:T(8,128)(2,1)} %fusion) | data formatting | bytes 67108864
  427.2 5.2 %copy.112 = bf16[1,32,2,4,32,32]{4,3,5,2,1,0:T(4,128)(2,1)S(1)} copy(bf16[1,32,2,4,32,32]{1,5,4,2,3,0:T(8,128)(2,1)} %bitcast_bitcast_fusion) | data formatting | bytes 1048576 | tf_op jit(solution)/shard_map/all_to_all | solution.py:106
  433.5 7.4 %convolution_bitcast_fusion.1 = f32[32,32,2,12,128]{4,1,3,2,0:T(8,128)} fusion(bf16[2,12,128,2,128]{4,2,1,0,3:T(8,128)(2,1)} %bitcast.152, bf16[32,2,128,32,1,1]{2,3,1,0,4,5:T(8,128)(2,1)S(1)} %reshape.229), kind=kOutput, calls=%fused_computation.16 | convolution fusion | flops 1610612736 | bytes 14680064 | tf_op jit(solution)/shard_map/pcht,mch->ptm/dot_general | solution.py:32
  440.9 9.1 %slice_bitcast_fusion.15 = (f32[32,32,2,128]{3,1,2,0:T(8,128)S(1)}, f32[32,32,2,128]{3,1,2,0:T(8,128)S(1)}, f32[32,32,2,128]{3,1,2,0:T(8,128)S(1)}, f32[32,32,2,...) fusion(f32[32,32,2,12,128]{4,1,3,2,0:T(8,128)} %convolution_bit, ...), kind=kLoop, calls=%fused_computation.54 | loop fusion | bytes 25165824 | tf_op jit(solution)/shard_map/squeeze | solution.py:37
  450.0 5.0 %add_bitcast_fusion = f32[32,2,43,128]{3,2,1,0:T(8,128)S(1)} fusion(f32[32,32,2,128]{3,1,2,0:T(8,128)} %get-tuple-element.22, f32[32,32,2,128]{3,1,2,0:T(8,128)} %get-tuple-element.23, f32[32,32,2,128]{3,1,2,0:T(8,128)S(1)} %get-tuple-element.13, f32[32,32,2,128]{3,1,2,0:T(8,128)S(1)} %get-tuple-element.14, f32[32,32,2,128]{3,1,2,0:T(8,128)S(1)} %get-tuple-element.15, ...), kind=kLoop, calls=%fused_computation.33 | loop fusion | flops 3874816 | bytes 13991936 | tf_op jit(solution)/shard_map/transpose | solution.py:39
  (63 shorter events, 42.4 us)
Async XLA Ops:
  7.2 187.1 %all-gather.2.cloned.1.call-start = ((), (), s32[]{:S(2)}) async-start(), calls=%async_computation.2 | async-start | bytes 20971520 | tf_op jit(solution)/shard_map/all_gather | solution.py:70
  11.7 4.2 copy-start.4
  30.2 4.8 %copy-start.3 = (bf16[64,2,32,1536]{3,0,1,2:T(8,128)(2,1)}, bf16[64,2,32,1536]{3,0,1,2:T(8,128)(2,1)S(1)}, u32[]{:S(2)}) copy-start(bf16[64,2,32,1536]{3,0,1,2:T(8,128)(2,1)S(1)} %copy_dynamic-update-slice_fusion) | copy-start | bytes 37748740
  82.6 6.6 %copy-start.5 = (s32[1024]{0:T(1024)S(1)}, s32[1024]{0:T(1024)}, u32[]{:S(2)}) copy-start(s32[1024]{0:T(1024)} %param.8) | copy-start | bytes 12292
  82.6 10.9 %copy-start.7 = (s32[256,1]{0,1:T(1,128)S(1)}, s32[256,1]{0,1:T(1,128)}, u32[]{:S(2)}) copy-start(s32[256,1]{0,1:T(1,128)} %param.11) | copy-start | bytes 3076
  82.6 11.0 %copy-start.6 = (s32[4]{0:T(128)S(1)}, s32[4]{0:T(128)}, u32[]{:S(2)}) copy-start(s32[4]{0:T(128)} %param.9) | copy-start | bytes 52
  230.9 3.4 copy-start
  234.4 66.6 %copy-start.1 = (bf16[1024,2,32,32]{0,3,1,2:T(8,128)(2,1)}, bf16[1024,2,32,32]{0,3,1,2:T(8,128)(2,1)S(1)}, u32[]{:S(2)}) copy-start(bf16[1024,2,32,32]{0,3,1,2:T(8,128)(2,1)S(1)} %broadcast_select_fusion) | copy-start | bytes 12582916
  234.4 2.7 copy-start.8
  311.8 112.5 %all-to-all-start.1 = ((bf16[4,2,32768]{2,1,0:T(2,128)(2,1)}), bf16[4,2,32768]{2,1,0:T(2,128)(2,1)S(1)}, u32[]{:S(2)}, u32[]{:S(2)}) async-start(bf16[4,2,32768]{2,1,0:T(2,128)(2,1)} %reshape.239), calls=%async_computation.1 | async-start | bytes 1048576 | tf_op jit(solution)/shard_map/all_to_all | solution.py:106
  316.4 15.5 %copy-start.2 = (bf16[2,32,1024,32]{2,3,0,1:T(8,128)(2,1)S(1)}, bf16[2,32,1024,32]{2,3,0,1:T(8,128)(2,1)}, u32[]{:S(2)}) copy-start(bf16[2,32,1024,32]{2,3,0,1:T(8,128)(2,1)} %fusion.78) | copy-start | bytes 12582916
Sparse Core Ops, SparseCore 0:
  89.2 104.9 all-gather.1
where the time goes:
time: 469 us; the launch traced here: 464 us
  matrix products  132 us (28%)
  local copies, waits for them, and re-layouts  131 us (28%)
  waiting for transfers between devices  94.4 us (20%)
  other arithmetic  55.3 us (12%)
  blocking collectives  32 us (7%)
  between operations  14.9 us (3%)
    all_gather x1, waiting for transfers between devices, local(): gathered = lax.all_gather(turned, 'sub', axis=2, tiled=True)  94.3 us
    unnamed x34, local copies, waits for them, and re-layouts  48.3 us
    gather x2, local copies, waits for them, and re-layouts, local(): by_id = jnp.take(gathered, order, axis=2)  36.6 us
    convert_element_type x1, other arithmetic, local(): (jnp.stack([real_part, imag_part], axis=1) / total).astype(jnp.bfloat16)  33.5 us
    dot_general x1, matrix products, local(): jnp.einsum('xbi,cxit->cxbt', weight_sin, by_id, preferred_element_type=jn...  32.1 us
    all_to_all x1, blocking collectives, local(): lax.all_to_all(spectra, 'chan', split_axis=1, concat_axis=2, tiled=True)  32 us
    dot_general x1, matrix products, local(): jnp.einsum('xbi,cxit->cxbt', weight_cos, by_id, preferred_element_type=jn...  31.8 us
    dot_general x1, matrix products, local(): jnp.einsum('xit,xjt->xij', mine[0], by_id[1], preferred_element_type=jnp....  21.7 us
  transfers between devices with their start and end apart: 2, of which 1 were waited for; matrix products, arithmetic and copies ran while one was open for 26% of the time, Pallas kernels for 0%

commit v1 on v0

--- a/solution.py
+++ b/solution.py
@@ -67,7 +67,13 @@
     spectra = filtered.reshape(2, chans, inp_dev, spectra_n).astype(jnp.bfloat16)
     slot_of = jnp.zeros((inputs,), jnp.int32).at[input_id].set(jnp.arange(inputs, dtype=jnp.int32))
     turned = lax.all_to_all(spectra, "chan", split_axis=1, concat_axis=2, tiled=True)
-    gathered = lax.all_gather(turned, "sub", axis=2, tiled=True)
+    size = lax.axis_size("sub")
+    current, blocks = (turned, [turned])
+    for _ in range(size - 1):
+        current = lax.ppermute(current, "sub", [(i, (i + 1) % size) for i in range(size)])
+        blocks.insert(0, current)
+    line = jnp.concatenate(blocks, axis=2)
+    gathered = jnp.roll(line, (lax.axis_index("sub") + 1) * turned.shape[2], axis=2)
     chan_part = slot_of // (n_sub * inp_dev)
     sub_part = slot_of // inp_dev % n_sub
     order = (sub_part * n_chan + chan_part) * inp_dev + slot_of % inp_dev

time: 469 us -> 420 us (0.90)
  waiting for transfers between devices: 94.4 us -> 31.9 us
  local copies, waits for them, and re-layouts: 131 us -> 159 us
  between operations: 14.9 us -> 1.56 us
    all_gather x1 -> x0, waiting for transfers between devices: 94.3 us -> none  [local(): gathered = lax.all_gather(turned, 'sub', axis=2, tiled=True)]
    ppermute x0 -> x3, waiting for transfers between devices: none -> 31.9 us  [local(): lax.ppermute(current, 'sub', [(i, (i + 1) % size) for i in range(size)])]
    unnamed x34 -> x42, local copies, waits for them, and re-layouts: 48.3 us -> 72.4 us
  transfers between devices with their start and end apart: 2 -> 4, of which waited for: 1 -> 3; matrix products, arithmetic and copies ran while one was open for 26% -> 29% of each run, Pallas kernels for 0% -> 0%
where the time goes in v1:
time: 420 us; the launch traced here: 415 us
  local copies, waits for them, and re-layouts  159 us (38%)
  matrix products  132 us (31%)
  other arithmetic  55.3 us (13%)
  blocking collectives  32 us (8%)
  waiting for transfers between devices  31.9 us (8%)
    unnamed x42, local copies, waits for them, and re-layouts  72.4 us
    gather x2, local copies, waits for them, and re-layouts, local(): by_id = jnp.take(gathered, order, axis=2)  36.6 us
    convert_element_type x1, other arithmetic, local(): (jnp.stack([real_part, imag_part], axis=1) / total).astype(jnp.bfloat16)  33.5 us
    dot_general x1, matrix products, local(): jnp.einsum('xbi,cxit->cxbt', weight_sin, by_id, preferred_element_type=jn...  32.1 us
    all_to_all x1, blocking collectives, local(): lax.all_to_all(spectra, 'chan', split_axis=1, concat_axis=2, tiled=True)  32 us
    ppermute x3, waiting for transfers between devices, local(): lax.ppermute(current, 'sub', [(i, (i + 1) % size) for i in range(size)])  31.9 us
    dot_general x1, matrix products, local(): jnp.einsum('xbi,cxit->cxbt', weight_cos, by_id, preferred_element_type=jn...  31.8 us
    dot_general x1, matrix products, local(): jnp.einsum('xit,xjt->xij', mine[0], by_id[1], preferred_element_type=jnp....  21.7 us
  transfers between devices with their start and end apart: 4, of which 3 were waited for; matrix products, arithmetic and copies ran while one was open for 29% of the time, Pallas kernels for 0%

profile of v1, /device:TPU:0, one launch (start us, length us, event | category | flops | bytes accessed | tf_op | source)
XLA Modules:
  0.0 414.9 jit_solution(3495637298301646917)
XLA Ops:
  9.4 4.7 %negate_convert_fusion.1 = (bf16[1536,128]{1,0:T(8,128)(2,1)S(1)}, bf16[1536,128]{1,0:T(8,128)(2,1)S(1)}, bf16[1536,128]{1,0:T(8,128)(2,1)S(1)}) fusion(s32[1536]{0:T(1024)S(1)} %add_select_fusion.3, f32[1536]{0:T(1024)S(1)} %copy-done.4), kind=kLoop, calls=%fused_computation.79 | loop fusion | flops 3932160 | bytes 1191936 | tf_op jit(solution)/shard_map/convert.13
  23.6 4.8 %copy-done.3 = bf16[64,2,32,1536]{3,0,1,2:T(8,128)(2,1)} copy-done((bf16[64,2,32,1536]{3,0,1,2:T(8,128)(2,1)}, bf16[64,2,32,1536]{3,0,1,2:T(8,128)(2,1)S(1)}, u32[]{:S(2)}) %copy-start.3) | copy-done | bytes 12582936
  28.5 8.3 %fusion.15 = bf16[256,64,32]{0,1,2:T(8,128)(2,1)S(1)} fusion(bf16[2,1536,256,1]{2,1,0,3:T(8,128)(2,1)S(1)} %bitcast.153, bf16[64,2,32,1536]{3,0,1,2:T(8,128)(2,1)} %copy-done.3, f32[32]{0:T(128)S(1)} %compare_convert_fusion), kind=kOutput, calls=%fused_computation.28 | convolution fusion | flops 3222274048 | bytes 15204480 | tf_op jit(solution)/shard_map/icth,chm->mit/dot_general | solution.py:65
  41.0 32.0 %all_to_all.33 = bf16[4,2,65536]{2,1,0:T(2,128)(2,1)} all-to-all(bf16[4,2,65536]{2,1,0:T(2,128)(2,1)S(1)} %reshape.237), channel_id=1, replica_groups=mesh['grp'=2,'chan'=4,'sub'=4] {'chan'}, dimensions={0} | all-to-all | bytes 2097152 | tf_op jit(solution)/shard_map/all_to_all | solution.py:69
  83.6 14.2 %collective-permute-done = bf16[2,32,256,32]{2,3,1,0:T(8,128)(2,1)S(1)} collective-permute-done((bf16[2,32,256,32]{2,3,1,0:T(8,128)(2,1)S(1)}, bf16[2,32,256,32]{2,3,1,0:T(8,128)(2,1)S(1)}, u32[]{:S(2)}, u32[]{:S(2)}) %collective-permute-start) | collective-permute-done | bytes 1048608 | tf_op jit(solution)/shard_map/ppermute | solution.py:73
  97.8 4.3 %scatter_custom_fusion = s32[1024]{0:T(1024)S(1)} fusion(s32[1024]{0:T(1024)S(1)} %compare_select_fusion.1, s32[1024]{0:T(1024)S(1)} %iota.42, s32[]{:T(128)} %constant.132.clone.1), kind=kCustom, calls=%fused_computation.142 | custom fusion | bytes 4100 | tf_op jit(solution)/shard_map/scatter | solution.py:68
  103.1 8.9 %collective-permute-done.1 = bf16[2,32,256,32]{2,3,1,0:T(8,128)(2,1)S(1)} collective-permute-done((bf16[2,32,256,32]{2,3,1,0:T(8,128)(2,1)S(1)}, bf16[2,32,256,32]{2,3,1,0:T(8,128)(2,1)S(1)}, u32[]{:S(2)}, u32[]{:S(2)}) %collective-permute-start.1) | collective-permute-done | bytes 1048608 | tf_op jit(solution)/shard_map/ppermute | solution.py:73
  112.1 4.1 negate_convert_fusion
  117.5 8.7 %collective-permute-done.2 = bf16[2,32,256,32]{2,3,1,0:T(8,128)(2,1)S(1)} collective-permute-done((bf16[2,32,256,32]{2,3,1,0:T(8,128)(2,1)S(1)}, bf16[2,32,256,32]{2,3,1,0:T(8,128)(2,1)S(1)}, u32[]{:S(2)}, u32[]{:S(2)}) %collective-permute-start.2) | collective-permute-done | bytes 1048608 | tf_op jit(solution)/shard_map/ppermute | solution.py:73
  130.0 23.0 %copy.164 = bf16[2,32,1024,32]{3,1,2,0:T(8,128)(2,1)} copy(bf16[2,32,1024,32]{2,3,1,0:T(8,128)(2,1)} %constant_dynamic-slice_fusion.1) | data formatting | bytes 8388608
  153.0 19.2 %gather_fusion = bf16[1024,2,32,32]{3,2,1,0:T(8,128)(2,1)} fusion(bf16[2,32,1024,32]{3,1,2,0:T(8,128)(2,1)} %copy.164, s32[1024]{0:T(1024)S(1)} %broadcast_clamp_fusion), kind=kCustom, calls=%fused_computation | custom fusion | bytes 8392704 | tf_op jit(solution)/shard_map/jit(_take)/gather | solution.py:80
  172.2 17.5 %copy.111 = bf16[1024,2,32,32]{0,3,1,2:T(8,128)(2,1)} copy(bf16[1024,2,32,32]{3,2,1,0:T(8,128)(2,1)} %gather_fusion) | data formatting | bytes 8388608 | tf_op jit(solution)/shard_map/jit(_take)/gather | solution.py:80
  195.7 31.8 %fusion.21 = f32[2,32,64,32]{2,3,0,1:T(8,128)S(1)} fusion(s32[32]{0:T(128)S(1)} %iota_add_fusion, s32[64,1024]{1,0:T(8,128)S(1)} %copy-done.8, bf16[1024,2,32,32]{0,3,1,2:T(8,128)(2,1)S(1)} %broadcast_select_fusion), kind=kOutput, calls=%fused_computation.35 | convolution fusion | flops 301989888 | bytes 4980864 | tf_op jit(solution)/shard_map/xbi,cxit->cxbt/dot_general | solution.py:96
  227.5 32.1 %fusion.18 = f32[2,32,64,32]{2,3,0,1:T(8,128)S(1)} fusion(s32[32]{0:T(128)S(1)} %iota_add_fusion, s32[64,1024]{1,0:T(8,128)S(1)} %copy-done.8, bf16[1024,2,32,32]{0,3,1,2:T(8,128)(2,1)S(1)} %broadcast_select_fusion), kind=kOutput, calls=%fused_computation.34 | convolution fusion | flops 301989888 | bytes 4980864 | tf_op jit(solution)/shard_map/xbi,cxit->cxbt/dot_general | solution.py:97
  266.0 4.5 %reshape.239 = bf16[4,2,32768]{2,1,0:T(2,128)(2,1)} reshape(bf16[4,2,32,32,32]{4,3,2,1,0:T(8,128)(2,1)} %bitcast.150) | data formatting | bytes 1048576
  274.0 15.5 %convolution_bitcast_fusion = f32[32,1,256,1024]{3,2,0,1:T(8,128)} fusion(bf16[2,32,256,32]{2,3,0,1:T(8,128)(2,1)S(1)} %dynamic-slice_bitcast_fusion, bf16[1024,2,32,32]{0,3,1,2:T(8,128)(2,1)} %copy-done.1), kind=kOutput, calls=%fused_computation.8 | convolution fusion | flops 1073741824 | bytes 38797312 | tf_op jit(solution)/shard_map/cxit,cxjt->xij/dot_general | solution.py:83
  289.4 14.0 %fusion.14 = f32[32,256,1024]{2,1,0:T(8,128)} fusion(bf16[2,32,1024,32]{2,3,0,1:T(8,128)(2,1)S(1)} %copy-done.2, bf16[2,32,256,32]{2,3,0,1:T(8,128)(2,1)S(1)} %dynamic-slice_bitcast_fusion), kind=kOutput, calls=%fused_computation.26 | convolution fusion | flops 536870912 | bytes 36175872 | tf_op jit(solution)/shard_map/xit,xjt->xij/dot_general | solution.py:84
  303.5 21.7 %subtract_bitcast_fusion = f32[32,1,256,1024]{3,2,0,1:T(8,128)} fusion(f32[32,256,1024]{2,1,0:T(8,128)} %fusion.14, bf16[2,32,1024,32]{2,3,0,1:T(8,128)(2,1)S(1)} %copy-done.2, bf16[2,32,256,32]{2,3,0,1:T(8,128)(2,1)S(1)} %dynamic-slice_bitcast_fusion), kind=kOutput, calls=%fused_computation.4 | convolution fusion | flops 545259520 | bytes 69730304 | tf_op jit(solution)/shard_map/xit,xjt->xij/dot_general | solution.py:85
  325.1 33.5 %fusion = bf16[32,2,256,1024]{3,2,0,1:T(8,128)(2,1)} fusion(f32[32,1,256,1024]{3,2,0,1:T(8,128)} %subtract_bitcast_fusion, f32[32,1,256,1024]{3,2,0,1:T(8,128)} %convolution_bitcast_fusion, f32[]{:T(128)} %convert_reduce_fusion.1), kind=kLoop, calls=%fused_computation.3 | loop fusion | flops 50331648 | bytes 100663296 | tf_op jit(solution)/shard_map/convert_element_type | solution.py:88
  358.7 23.2 %copy.128 = bf16[32,2,256,1024]{3,2,1,0:T(8,128)(2,1)} copy(bf16[32,2,256,1024]{3,2,0,1:T(8,128)(2,1)} %fusion) | data formatting | bytes 67108864
  384.8 5.2 %copy.114 = bf16[1,32,2,4,32,32]{4,3,5,2,1,0:T(4,128)(2,1)S(1)} copy(bf16[1,32,2,4,32,32]{1,5,4,2,3,0:T(8,128)(2,1)} %bitcast_bitcast_fusion) | data formatting | bytes 1048576 | tf_op jit(solution)/shard_map/all_to_all | solution.py:112
  391.1 7.4 %convolution_bitcast_fusion.1 = f32[32,32,2,12,128]{4,1,3,2,0:T(8,128)} fusion(bf16[2,12,128,2,128]{4,2,1,0,3:T(8,128)(2,1)} %bitcast.152, bf16[32,2,128,32,1,1]{2,3,1,0,4,5:T(8,128)(2,1)S(1)} %reshape.229), kind=kOutput, calls=%fused_computation.16 | convolution fusion | flops 1610612736 | bytes 14680064 | tf_op jit(solution)/shard_map/pcht,mch->ptm/dot_general | solution.py:32
  398.5 9.1 %slice_bitcast_fusion.15 = (f32[32,32,2,128]{3,1,2,0:T(8,128)S(1)}, f32[32,32,2,128]{3,1,2,0:T(8,128)S(1)}, f32[32,32,2,128]{3,1,2,0:T(8,128)S(1)}, f32[32,32,2,...) fusion(f32[32,32,2,12,128]{4,1,3,2,0:T(8,128)} %convolution_bit, ...), kind=kLoop, calls=%fused_computation.54 | loop fusion | bytes 25165824 | tf_op jit(solution)/shard_map/squeeze | solution.py:37
  407.6 5.0 %add_bitcast_fusion = f32[32,2,43,128]{3,2,1,0:T(8,128)S(1)} fusion(f32[32,32,2,128]{3,1,2,0:T(8,128)} %get-tuple-element.22, f32[32,32,2,128]{3,1,2,0:T(8,128)} %get-tuple-element.23, f32[32,32,2,128]{3,1,2,0:T(8,128)S(1)} %get-tuple-element.13, f32[32,32,2,128]{3,1,2,0:T(8,128)S(1)} %get-tuple-element.14, f32[32,32,2,128]{3,1,2,0:T(8,128)S(1)} %get-tuple-element.15, ...), kind=kLoop, calls=%fused_computation.33 | loop fusion | flops 3874816 | bytes 13991936 | tf_op jit(solution)/shard_map/transpose | solution.py:39
  (77 shorter events, 60.7 us)
Async XLA Ops:
  5.1 4.2 %copy-start.4 = (f32[1536]{0:T(1024)S(1)}, f32[1536]{0:T(1024)}, u32[]{:S(2)}) copy-start(f32[1536]{0:T(1024)} %param.7) | copy-start | bytes 18436
  23.6 4.8 %copy-start.3 = (bf16[64,2,32,1536]{3,0,1,2:T(8,128)(2,1)}, bf16[64,2,32,1536]{3,0,1,2:T(8,128)(2,1)S(1)}, u32[]{:S(2)}) copy-start(bf16[64,2,32,1536]{3,0,1,2:T(8,128)(2,1)S(1)} %copy_dynamic-update-slice_fusion) | copy-start | bytes 37748740
  39.3 58.6 %copy-start.5 = (s32[1024]{0:T(1024)S(1)}, s32[1024]{0:T(1024)}, u32[]{:S(2)}) copy-start(s32[1024]{0:T(1024)} %param.8) | copy-start | bytes 12292
  39.3 62.9 %copy-start.7 = (s32[256,1]{0,1:T(1,128)S(1)}, s32[256,1]{0,1:T(1,128)}, u32[]{:S(2)}) copy-start(s32[256,1]{0,1:T(1,128)} %param.11) | copy-start | bytes 3076
  39.3 63.0 %copy-start.6 = (s32[4]{0:T(128)S(1)}, s32[4]{0:T(128)}, u32[]{:S(2)}) copy-start(s32[4]{0:T(128)} %param.9) | copy-start | bytes 52
  83.5 14.3 %collective-permute-start = (bf16[2,32,256,32]{2,3,1,0:T(8,128)(2,1)S(1)}, bf16[2,32,256,32]{2,3,1,0:T(8,128)(2,1)S(1)}, u32[]{:S(2)}, u32[]{:S(2)}) collective-permute-start(bf16[2,32,256,32]{2,3,1,0:T(8,128)(2,1)S(1)} %all_to_all.27), channel_id=1, source_target_pairs={{0,1},{1,2},{2,3},{3,0},{4,5},{5,6},{6,7},{7,4},{8,9},{9,10},{10,1... | collective-permute-start | bytes 3145736 | tf_op jit(solution)/shard_map/ppermute | solution.py:73
  97.8 14.2 %collective-permute-start.1 = (bf16[2,32,256,32]{2,3,1,0:T(8,128)(2,1)S(1)}, bf16[2,32,256,32]{2,3,1,0:T(8,128)(2,1)S(1)}, u32[]{:S(2)}, u32[]{:S(2)}) collective-permute-start(bf16[2,32,256,32]{2,3,1,0:T(8,128)(2,1)S(1)} %collective-permute-done), channel_id=1, source_target_pairs={{0,1},{1,2},{2,3},{3,0},{4,5},{5,6},{6,7},{7,4},{8,9},{9,10},{10,1... | collective-permute-start | bytes 3145736 | tf_op jit(solution)/shard_map/ppermute | solution.py:73
  112.0 14.2 %collective-permute-start.2 = (bf16[2,32,256,32]{2,3,1,0:T(8,128)(2,1)S(1)}, bf16[2,32,256,32]{2,3,1,0:T(8,128)(2,1)S(1)}, u32[]{:S(2)}, u32[]{:S(2)}) collective-permute-start(bf16[2,32,256,32]{2,3,1,0:T(8,128)(2,1)S(1)} %collective-permute-done.1), channel_id=1, source_target_pairs={{0,1},{1,2},{2,3},{3,0},{4,5},{5,6},{6,7},{7,4},{8,9},{9,10},{10,1... | collective-permute-start | bytes 3145736 | tf_op jit(solution)/shard_map/ppermute | solution.py:73
  189.6 3.4 copy-start
  189.6 6.1 %copy-start.8 = (s32[64,1024]{1,0:T(8,128)S(1)}, s32[64,1024]{1,0:T(8,128)}, u32[]{:S(2)}) copy-start(s32[64,1024]{1,0:T(8,128)} %param.10) | copy-start | bytes 786436
  193.1 66.5 %copy-start.1 = (bf16[1024,2,32,32]{0,3,1,2:T(8,128)(2,1)}, bf16[1024,2,32,32]{0,3,1,2:T(8,128)(2,1)S(1)}, u32[]{:S(2)}) copy-start(bf16[1024,2,32,32]{0,3,1,2:T(8,128)(2,1)S(1)} %broadcast_select_fusion) | copy-start | bytes 12582916
  270.5 111.5 %all-to-all-start.1 = ((bf16[4,2,32768]{2,1,0:T(2,128)(2,1)}), bf16[4,2,32768]{2,1,0:T(2,128)(2,1)S(1)}, u32[]{:S(2)}, u32[]{:S(2)}) async-start(bf16[4,2,32768]{2,1,0:T(2,128)(2,1)} %reshape.239), calls=%async_computation.1 | async-start | bytes 1048576 | tf_op jit(solution)/shard_map/all_to_all | solution.py:112
  273.9 15.5 %copy-start.2 = (bf16[2,32,1024,32]{2,3,0,1:T(8,128)(2,1)S(1)}, bf16[2,32,1024,32]{2,3,0,1:T(8,128)(2,1)}, u32[]{:S(2)}) copy-start(bf16[2,32,1024,32]{2,3,0,1:T(8,128)(2,1)} %fusion.79) | copy-start | bytes 12582916
